TPU v7x, 32 devices: a whole 2x2x4 slice. The times are simulated.
32 devices in a mesh: pipe: 4 (over y, x), ctx: 8 (over z, core).
Axes of the slice: x: 2, y: 2, z: 4, core: 2. Of those that a mesh axis runs over, the one named last changes fastest.
Arguments:
- tokens: bfloat16 [4, 1024, 8192], P('pipe', 'ctx')
- queries: bfloat16 [4, 1024, 4096], P('pipe', 'ctx')
- key_weight: bfloat16 [8192, 512], P(('pipe', 'ctx'))
- value_weight: bfloat16 [8192, 512], P(('pipe', 'ctx')), may hold values from -0.0625 to 0.0625
- block_order: int32 [16], replicated, may hold values from 0 to 15, as said below
Outputs:
- attended: bfloat16 [4, 1024, 4096], P('pipe', 'ctx')
Inputs may be any that keep to these rules, and one draw needn't show every extreme that they name: `block_order`: each of the 16 half-blocks appears once.
All inputs are finite; a program needn't handle non-finite values.
Results may differ from a plain program's by a relative error of at most 0.0056.
The roundings to bfloat16 on the way count: a program that leaves them out, or rounds other values in their place, can miss the bound.
Values may be sent and summed in bfloat16 or wider, within the bound.
A program may use at most 64 MiB of HBM per device.

v0:
```python
import functools

import jax
import jax.numpy as jnp
from jax import lax
from jax.experimental import pallas as pl
from jax.experimental.pallas import tpu as pltpu
from jax.sharding import PartitionSpec as P

HEAD_SIZE = 128
FIRST = 0
LOG2E = 1.4426950408889634
MESH = pl.DeviceIdType.MESH
PARTIAL = jnp.bfloat16


class Gather:
    def __init__(self, buf, rows, send, recv, lines):
        self.buf, self.rows, self.send_sems, self.recv_sems, self.lines = buf, rows, send, recv, lines
        self.me = lax.axis_index("ctx")
        self.line = self.me // 2
        self.core = self.me % 2
        self.partner = self.me + 1 - 2 * self.core

    def copy(self, g, origin, way):
        target = (self.me + 2, self.me - 2, self.partner)[way]
        return self.block_copy(g, origin, self.send_sems.at[g, origin // 2, way], target)

    def block_copy(self, g, origin, send_sem, target):
        block = self.buf.at[g, pl.ds(pl.multiple_of(origin * self.rows, self.rows), self.rows), :]
        return pltpu.make_async_remote_copy(
            src_ref=block,
            dst_ref=block,
            send_sem=send_sem,
            recv_sem=self.recv_sems.at[g, origin],
            device_id={"ctx": target},
            device_id_type=MESH,
        )

    def own(self, g):
        @pl.when(self.line < self.lines - 1)
        def _():
            self.copy(g, self.me, 0).start()

        @pl.when(self.line > 0)
        def _():
            self.copy(g, self.me, 1).start()

        self.copy(g, self.me, 2).start()

    def forward(self, g, start=1, stop=None):
        @pl.loop(start, self.lines if stop is None else stop)
        def _(hop):
            @pl.when(self.line >= hop)
            def _():
                origin = self.me - 2 * hop
                self.copy(g, origin, 2).wait_recv()

                @pl.when(self.line < self.lines - 1)
                def _():
                    self.copy(g, origin, 0).start()

                self.copy(g, origin, 2).start()

            @pl.when(self.line + hop < self.lines)
            def _():
                origin = self.me + 2 * hop
                self.copy(g, origin, 2).wait_recv()

                @pl.when(self.line > 0)
                def _():
                    self.copy(g, origin, 1).start()

                self.copy(g, origin, 2).start()

    def join(self, g):
        @pl.loop(0, self.lines)
        def _(line):
            self.copy(g, 2 * line + 1 - self.core, 2).wait_recv()

    def drain(self, chunks):
        @pl.loop(0, chunks)
        def _(g):
            @pl.loop(0, self.lines)
            def _(line):
                origin = 2 * line + self.core

                @pl.when((line <= self.line) & (self.line < self.lines - 1))
                def _():
                    self.copy(g, origin, 0).wait_send()

                @pl.when((line >= self.line) & (self.line > 0))
                def _():
                    self.copy(g, origin, 1).wait_send()

                self.copy(g, origin, 2).wait_send()


class Direct(Gather):
    def sent(self, g, step):
        line = lax.rem(self.line + step, self.lines)
        return self.block_copy(g, self.me, self.send_sems.at[g, step - 1, 0], 2 * line + self.core)

    def relay(self, g, line):
        return self.block_copy(g, 2 * line + self.core, self.send_sems.at[g, line, 1], self.partner)

    def own(self, g):
        for step in range(1, self.lines):
            self.sent(g, step).start()
        self.relay(g, self.line).start()

    def forward(self, g):
        @pl.loop(1, self.lines)
        def _(step):
            line = lax.rem(self.line + step, self.lines)
            self.relay(g, line).wait_recv()
            self.relay(g, line).start()

    def drain(self, chunks):
        @pl.loop(0, chunks)
        def _(g):
            @pl.loop(1, self.lines)
            def _(step):
                self.sent(g, step).wait_send()

            @pl.loop(0, self.lines)
            def _(line):
                self.relay(g, line).wait_send()


def kernel(
    pipes, ctxs, half,
    tok, qry, kw, vw, order, out,
    wbuf, xbuf, pout, pin, mine, kvbuf, qbuf, obuf,
    w_send, w_recv, kv_send, kv_recv, x_send, x_recv, p_send, p_recv, local, out_sem,
):
    chunks = wbuf.shape[0]
    rows = qbuf.shape[0]
    deep = kw.shape[0]
    slice_rows = xbuf.shape[2]
    lines = ctxs // 2
    group = qbuf.shape[1] // (chunks * HEAD_SIZE)
    seq = kvbuf.shape[1]
    pipe = lax.axis_index("pipe")
    me = lax.axis_index("ctx")
    weights = Gather(wbuf, deep, w_send, w_recv, lines)
    rows_kv = Direct(kvbuf, rows, kv_send, kv_recv, lines)

    def weight_copy(g, which):
        return pltpu.make_async_copy(
            (kw, vw)[which].at[:, pl.ds(g * HEAD_SIZE, HEAD_SIZE)],
            wbuf.at[g, pl.ds(pl.multiple_of(me * deep, deep), deep), pl.ds(which * HEAD_SIZE, HEAD_SIZE)],
            local.at[2 * g + which],
        )

    def own_tokens():
        return pltpu.make_async_copy(
            tok.at[0, :, pl.ds(pl.multiple_of(pipe * slice_rows, slice_rows), slice_rows)],
            xbuf.at[pipe],
            local.at[2 * chunks],
        )

    def own_queries():
        return pltpu.make_async_copy(qry.at[0], qbuf, local.at[2 * chunks + 1])

    def token_copy(d, to):
        return pltpu.make_async_remote_copy(
            src_ref=tok.at[0, :, pl.ds(pl.multiple_of(to * slice_rows, slice_rows), slice_rows)],
            dst_ref=xbuf.at[pipe],
            send_sem=x_send.at[d - 1],
            recv_sem=x_recv.at[d - 1],
            device_id={"pipe": to},
            device_id_type=MESH,
        )

    def token_wait(d):
        source = lax.rem(pipe + pipes - d, pipes)
        pltpu.make_async_remote_copy(
            src_ref=xbuf.at[source],
            dst_ref=xbuf.at[source],
            send_sem=x_send.at[d - 1],
            recv_sem=x_recv.at[d - 1],
            device_id={"pipe": source},
            device_id_type=MESH,
        ).wait_recv()

    def partial_copy(g, d):
        to = lax.rem(pipe + d, pipes)
        return pltpu.make_async_remote_copy(
            src_ref=pout.at[g, to],
            dst_ref=pin.at[g, d - 1],
            send_sem=p_send.at[g, d - 1],
            recv_sem=p_recv.at[g, d - 1],
            device_id={"pipe": to},
            device_id_type=MESH,
        )

    for g in range(chunks):
        for which in range(2):
            weight_copy(g, which).start()
    own_tokens().start()
    own_queries().start()

    barrier = pltpu.get_barrier_semaphore()
    for d in range(1, pipes):
        pl.semaphore_signal(barrier, inc=1, device_id={"pipe": lax.rem(pipe + d, pipes)}, device_id_type=MESH)
    pl.semaphore_signal(barrier, inc=1, device_id={"ctx": weights.partner}, device_id_type=MESH)
    for step in range(1, lines):
        to = 2 * lax.rem(weights.line + step, lines) + weights.core
        pl.semaphore_signal(barrier, inc=1, device_id={"ctx": to}, device_id_type=MESH)
    pl.semaphore_wait(barrier, pipes + lines - 1)

    def own_weights(g):
        weight_copy(g, 0).wait()
        weight_copy(g, 1).wait()
        weights.own(g)

    def multiply(g):
        weights.join(g)
        left = xbuf[...].reshape(pipes * rows, slice_rows)
        product = jnp.dot(left, wbuf[g], preferred_element_type=jnp.float32)
        pout[g] = product.reshape(pipes, rows, 2 * HEAD_SIZE).astype(pout.dtype)
        for d in range(1, pipes):
            partial_copy(g, d).start()
        for row in range(pipes):

            @pl.when(pipe == row)
            def _():
                mine[g] = product[row * rows : (row + 1) * rows]

    def total(g):
        value = mine[g]
        for d in range(1, pipes):
            partial_copy(g, d).wait_recv()
            value = value + pin[g, d - 1].astype(jnp.float32)
        kvbuf[g, pl.ds(pl.multiple_of(me * rows, rows), rows), :] = value.astype(jnp.bfloat16)
        rows_kv.own(g)

    lane = lax.broadcasted_iota(jnp.int32, (1, seq), 1)
    spot = jnp.zeros((1, seq), jnp.int32)
    for i in range(seq // half):
        spot = jnp.where(lane // half == i, order[i] * half, spot)
    key_position = spot + lane % half
    row = lax.broadcasted_iota(jnp.int32, (rows, 1), 0)
    spot = jnp.zeros((rows, 1), jnp.int32)
    per = rows // half
    for i in range(per):
        spot = jnp.where(row // half == i, order[me * per + i] * half, spot)
    own_position = spot + row % half

    factor = LOG2E / HEAD_SIZE**0.5

    def out_copy(g):
        columns = pl.ds(g * group * HEAD_SIZE, group * HEAD_SIZE)
        return pltpu.make_async_copy(obuf.at[:, columns], out.at[0, :, columns], out_sem.at[g])

    def attend(g):
        rows_kv.join(g)

        @pl.loop(0, group, unroll=2)
        def _(h):
            columns = pl.ds(pl.multiple_of((g * group + h) * HEAD_SIZE, HEAD_SIZE), HEAD_SIZE)
            keys = kvbuf[g, :, :HEAD_SIZE]
            values = kvbuf[g, :, HEAD_SIZE:]
            score = lax.dot_general(
                qbuf[:, columns], keys, (((1,), (1,)), ((), ())), preferred_element_type=jnp.float32
            )
            score = jnp.where(key_position <= own_position, score, -jnp.inf)
            largest = jnp.max(score, axis=1, keepdims=True)
            expo = jnp.exp2((score - largest) * factor)
            amount = jnp.sum(expo, axis=1, keepdims=True)
            summed = jnp.dot(expo.astype(jnp.bfloat16), values, preferred_element_type=jnp.float32)
            obuf[:, columns] = (summed / amount).astype(jnp.bfloat16)

        out_copy(g).start()

    def tokens_ready():
        own_tokens().wait()
        for d in range(1, pipes):
            token_wait(d)

    own_weights(0)
    for d in range(1, pipes):
        token_copy(d, lax.rem(pipe + d, pipes)).start()
    last = chunks - 1
    if last >= 1:
        own_weights(1)
    first = min(FIRST, last)
    for step in range(chunks + lines - 2):
        for hop in range(lines - 1, 0, -1):
            if 0 <= step - hop + 1 <= last:
                weights.forward(step - hop + 1, hop, hop + 1)
        if step + 2 <= last:
            own_weights(step + 2)
        done = step - (lines - 2)
        if done == first:
            tokens_ready()
            for g in range(done):
                multiply(g)
        if done >= first:
            if done == last and done >= 2:
                total(done - 2)
            multiply(done)
            if 2 <= done < last:
                total(done - 2)
    own_queries().wait()
    if last >= 1:
        total(last - 1)
    attended = max(last - 2, 0)
    for g in range(attended):
        rows_kv.forward(g)
        attend(g)
    total(last)
    for g in range(attended, last):
        rows_kv.forward(g)
        if g == last - 1:
            rows_kv.forward(last)
        attend(g)
    if last == 0:
        rows_kv.forward(last)
    attend(last)

    weights.drain(chunks)
    rows_kv.drain(chunks)
    for d in range(1, pipes):
        token_copy(d, lax.rem(pipe + d, pipes)).wait_send()
        for g in range(chunks):
            partial_copy(g, d).wait_send()
    for g in range(chunks):
        out_copy(g).wait()


def body(pipes, ctxs, tokens, queries, key_weight, value_weight, block_order):
    rows, width = tokens.shape[1:]
    deep, kv_width = key_weight.shape
    chunks = kv_width // HEAD_SIZE
    seq = rows * ctxs
    half = seq // block_order.shape[0]
    pair = 2 * HEAD_SIZE
    dma = pltpu.SemaphoreType.DMA
    any_space = pl.BlockSpec(memory_space=pl.ANY)
    return pl.pallas_call(
        functools.partial(kernel, pipes, ctxs, half),
        out_shape=jax.ShapeDtypeStruct(queries.shape, jnp.bfloat16),
        in_specs=[any_space] * 4 + [pl.BlockSpec(memory_space=pltpu.SMEM)],
        out_specs=any_space,
        scratch_shapes=[
            pltpu.VMEM((chunks, deep * ctxs, pair), jnp.bfloat16),
            pltpu.VMEM((pipes, rows, width // pipes), jnp.bfloat16),
            pltpu.VMEM((chunks, pipes, rows, pair), PARTIAL),
            pltpu.VMEM((chunks, pipes - 1, rows, pair), PARTIAL),
            pltpu.VMEM((chunks, rows, pair), jnp.float32),
            pltpu.VMEM((chunks, seq, pair), jnp.bfloat16),
            pltpu.VMEM(queries.shape[1:], jnp.bfloat16),
            pltpu.VMEM(queries.shape[1:], jnp.bfloat16),
            dma((chunks, ctxs // 2, 3)),
            dma((chunks, ctxs)),
            dma((chunks, ctxs // 2, 2)),
            dma((chunks, ctxs)),
            dma((pipes - 1,)),
            dma((pipes - 1,)),
            dma((chunks, pipes - 1)),
            dma((chunks, pipes - 1)),
            dma((2 * chunks + 2,)),
            dma((chunks,)),
        ],
        compiler_params=pltpu.CompilerParams(
            collective_id=0, has_side_effects=True, vmem_limit_bytes=60 * 1024 * 1024
        ),
    )(tokens, queries, key_weight, value_weight, block_order)


def solution(mesh):
    return jax.shard_map(
        functools.partial(body, mesh.shape["pipe"], mesh.shape["ctx"]),
        mesh=mesh,
        in_specs=(
            P("pipe", "ctx", None),
            P("pipe", "ctx", None),
            P(("pipe", "ctx"), None),
            P(("pipe", "ctx"), None),
            P(),
        ),
        out_specs=P("pipe", "ctx", None),
        check_vma=False,
    )
```

profile of v0, /device:TPU:0, one launch (start us, length us, event | category | flops | bytes accessed | tf_op | source)
XLA Modules:
  0.0 72.5 jit_solution(15694430224252748335)
XLA Ops:
  0.0 70.2 %shard_map.55 = bf16[1,128,4096]{2,1,0:T(8,128)(2,1)} custom-call(bf16[1,128,8192]{2,1,0:T(8,128)(2,1)} %tok.1, bf16[1,128,4096]{2,1,0:T(8,128)(2,1)} %qry.1, bf16[256,512]{1,0:T(8,128)(2,1)} %kw.1, bf16[256,512]{1,0:T(8,128)(2,1)} %vw.1, s32[16]{0:T(128)} %order.1), custom_call_target="tpu_custom_call" | custom-call | tf_op jit(solution)/shard_map/pallas_call | solution.py:342
  70.2 2.3 %copy.7 = bf16[1,128,4096]{2,1,0:T(8,128)(2,1)} copy(bf16[1,128,4096]{2,1,0:T(8,128)(2,1)} %shard_map.55) | data formatting | bytes 2097152
where the time goes:
time: 72.7 us; the launch traced here: 72.5 us
  Pallas kernels  70.2 us (97%)
  local copies, waits for them, and re-layouts  2.29 us (3%)
    pallas_call x1, Pallas kernels, body(): pl.pallas_call(functools.partial(kernel, pipes, ctxs, half), out_shape=ja...  70.2 us
    unnamed x1, local copies, waits for them, and re-layouts  2.29 us

commit v1 on v0

--- a/solution.py
+++ b/solution.py
@@ -257,7 +257,7 @@
     def attend(g):
         rows_kv.join(g)
 
-        @pl.loop(0, group, unroll=2)
+        @pl.loop(0, group, unroll=8)
         def _(h):
             columns = pl.ds(pl.multiple_of((g * group + h) * HEAD_SIZE, HEAD_SIZE), HEAD_SIZE)
             keys = kvbuf[g, :, :HEAD_SIZE]

time: 72.7 us -> 71.1 us (0.978)
  Pallas kernels: 70.2 us -> 68.7 us
    pallas_call x1, Pallas kernels: 70.2 us -> 68.7 us  [body(): pl.pallas_call(functools.partial(kernel, pipes, ctxs, half), out_shape=ja...]
where the time goes in v1:
time: 71.1 us; the launch traced here: 71 us
  Pallas kernels  68.7 us (97%)
  local copies, waits for them, and re-layouts  2.29 us (3%)
    pallas_call x1, Pallas kernels, body(): pl.pallas_call(functools.partial(kernel, pipes, ctxs, half), out_shape=ja...  68.7 us
    unnamed x1, local copies, waits for them, and re-layouts  2.29 us

profile of v1, /device:TPU:0, one launch (start us, length us, event | category | flops | bytes accessed | tf_op | source)
XLA Modules:
  0.0 71.0 jit_solution(15374719387491835478)
XLA Ops:
  0.0 68.7 %shard_map.55 = bf16[1,128,4096]{2,1,0:T(8,128)(2,1)} custom-call(bf16[1,128,8192]{2,1,0:T(8,128)(2,1)} %tok.1, bf16[1,128,4096]{2,1,0:T(8,128)(2,1)} %qry.1, bf16[256,512]{1,0:T(8,128)(2,1)} %kw.1, bf16[256,512]{1,0:T(8,128)(2,1)} %vw.1, s32[16]{0:T(128)} %order.1), custom_call_target="tpu_custom_call" | custom-call | tf_op jit(solution)/shard_map/pallas_call | solution.py:342
  68.7 2.3 %copy.7 = bf16[1,128,4096]{2,1,0:T(8,128)(2,1)} copy(bf16[1,128,4096]{2,1,0:T(8,128)(2,1)} %shard_map.55) | data formatting | bytes 2097152
